TPU v7x, 128 devices: a whole 4x4x4 slice. The times are simulated.
128 devices in a mesh: dp: 16 (over x, z_lo, core), tensor: 8 (over z_hi, y).
Axes of the slice: x: 4, y: 4, z: 4 (z_hi: 2, z_lo: 2; z = z_hi * 2 + z_lo), core: 2. Of those that a mesh axis runs over, the one named last changes fastest.
Arguments:
- inputs: bfloat16 [4096, 4096], P('dp', 'tensor'), may hold values from -6 to 6
- gate_pre: bfloat16 [4096, 14336], P('dp', 'tensor'), may hold values from -9 to 9
- up_pre: bfloat16 [4096, 14336], P('dp', 'tensor'), may hold values from -6 to 6
- out_grad: bfloat16 [4096, 4096], P('dp', 'tensor'), may hold values from -0.09375 to 0.09375
- down_weight: bfloat16 [14336, 4096], P('tensor'), may hold values from -0.09375 to 0.09375
Outputs:
- gate_wgrad: bfloat16 [4096, 14336], P('dp', 'tensor')
- up_wgrad: bfloat16 [4096, 14336], P('dp', 'tensor')
- in_cov: float32 [4096, 1024], P(('dp', 'tensor'))
- gate_cov: float32 [8, 1792, 896], P('tensor', 'dp')
- up_cov: float32 [8, 1792, 896], P('tensor', 'dp')
All inputs are finite; a program needn't handle non-finite values.
Results may differ from a plain program's by a relative error of at most 0.014.
Values may be sent and summed in bfloat16 or wider, within the bound.
A program may use at most 192 MiB of HBM per device.

v0:
```python
import jax
import jax.numpy as jnp
from jax import lax
from jax.sharding import PartitionSpec as P

BLK = 1024
HBLK = 896


def sent_together(arrays, axis, dim, along):
    both = jnp.concatenate(arrays, axis=along)
    whole, at, outs = (lax.all_gather(both, axis, axis=dim, tiled=True), 0, [])
    for a in arrays:
        outs.append(lax.slice_in_dim(whole, at, at + a.shape[along], axis=along))
        at += a.shape[along]
    return tuple(outs)


def split_up(x, dim, count):
    shape = x.shape
    tiles = x.reshape(*shape[:dim], count, shape[dim] // count, *shape[dim + 1 :])
    return jnp.moveaxis(tiles, dim, 0)


def summed_on_arrival(x, axis, dim):
    tiles = split_up(x, dim, lax.axis_size(axis))
    arrived = lax.all_to_all(tiles, axis, split_axis=0, concat_axis=0, tiled=True)
    return arrived.astype(jnp.float32).sum(axis=0)


def inner(left, right):
    return lax.dot_general(
        left, right, (((0,), (0,)), ((), ())), preferred_element_type=jnp.float32
    )


def on_device(inputs, gate_pre, up_pre, out_grad, down_weight):
    dp_count = lax.axis_size("dp")
    tp_count = lax.axis_size("tensor")
    dp_index = lax.axis_index("dp")
    tp_index = lax.axis_index("tensor")
    inputs_full, grad_full = sent_together((inputs, out_grad), "tensor", 1, 0)
    tok_rows = inputs_full.shape[0]
    width = inputs_full.shape[1]
    total_tokens = tok_rows * dp_count
    own_width = width // dp_count
    cov_rows = width // (dp_count * tp_count)
    block_count = width // BLK
    repeated = jnp.repeat(
        inputs_full.reshape(tok_rows, block_count, BLK), dp_count // block_count, axis=1
    )
    split = inputs_full.reshape(tok_rows, dp_count, own_width)
    x_owned = lax.all_to_all(split, "dp", split_axis=1, concat_axis=0, tiled=True).reshape(
        total_tokens, own_width
    )
    picked = inputs_full.reshape(tok_rows, dp_count, tp_count, cov_rows)
    picked = lax.dynamic_index_in_dim(picked, tp_index, 2, keepdims=False)
    term = jnp.einsum("tdr,tdb->drb", picked, repeated, preferred_element_type=jnp.float32)
    in_cov = summed_on_arrival(term.astype(jnp.bfloat16), "dp", 0)[0] / total_tokens
    hidden_grad = lax.dot_general(
        grad_full, down_weight, (((1,), (1,)), ((), ())), preferred_element_type=jnp.float32
    )
    gate = gate_pre.astype(jnp.float32)
    up = up_pre.astype(jnp.float32)
    sig = jax.nn.sigmoid(gate)
    gate_grad = (hidden_grad * up * sig * (1.0 + gate * (1.0 - sig))).astype(jnp.bfloat16)
    up_grad = (hidden_grad * gate * sig).astype(jnp.bfloat16)
    hidden = gate_grad.shape[1]
    hid_rows = hidden // dp_count
    row_start = dp_index * hid_rows
    block_start = row_start // HBLK * HBLK

    def accumulate_one(piece):
        wgrad = inner(x_owned, piece)
        own_cols = lax.dynamic_slice_in_dim(piece, row_start, hid_rows, 1)
        block_cols_h = lax.dynamic_slice_in_dim(piece, block_start, HBLK, 1)
        factor = inner(own_cols, block_cols_h)
        return (wgrad, factor)

    gate_sums = accumulate_one(lax.all_gather(gate_grad, "dp", axis=0, tiled=True))
    up_sums = accumulate_one(lax.all_gather(up_grad, "dp", axis=0, tiled=True))
    gate_wgrad = gate_sums[0].astype(jnp.bfloat16)
    up_wgrad = up_sums[0].astype(jnp.bfloat16)
    gate_cov = gate_sums[1].reshape(1, hid_rows, HBLK)
    up_cov = up_sums[1].reshape(1, hid_rows, HBLK)
    return (gate_wgrad, up_wgrad, in_cov, gate_cov, up_cov)


def solution(mesh):
    placed = (
        P("dp", "tensor"),
        P("dp", "tensor"),
        P("dp", "tensor"),
        P("dp", "tensor"),
        P("tensor", None),
    )
    return jax.shard_map(
        on_device,
        mesh=mesh,
        in_specs=placed,
        out_specs=(
            P("dp", "tensor"),
            P("dp", "tensor"),
            P(("dp", "tensor"), None),
            P("tensor", "dp", None),
            P("tensor", "dp", None),
        ),
        check_vma=False,
    )
```

profile of v0, /device:TPU:1, one launch (start us, length us, event | category | flops | bytes accessed | tf_op | source)
XLA Modules:
  0.0 319.3 jit_solution(9122356042220366269)
XLA Ops:
  7.2 1.2 copy.19
  8.4 1.1 copy.20
  9.5 0.8 pad_maximum_fusion
  10.4 75.0 %all-gather.4.cloned.1.call-done = bf16[512,4096]{0,1:T(8,128)(2,1)} async-done(((bf16[512,512]{0,1:T(8,128)(2,1)}), bf16[512,4096]{0,1:T(8,128)(2,1)}) %all-gather.4.cloned.1.call-update) | async-done | bytes 4194320 | tf_op jit(solution)/shard_map/all_gather | solution.py:12
  85.4 11.7 %fusion.13 = (bf16[256,1792]{1,0:T(8,128)(2,1)}, bf16[256,1792]{1,0:T(8,128)(2,1)}) fusion(bf16[256,1792]{1,0:T(8,128)(2,1)S(1)} %copy-done.3, bf16[256,1792]{1,0:T(8,128)(2,1)S(1)} %copy-done.4, bf16[1792,4096]{1,0:T(8,128)(2,1)} %param.9, bf16[512,4096]{0,1:T(8,128)(2,1)} %all-gather.4.cloned.1.call-done), kind=kOutput, calls=%fused_computation.19 | convolution fusion | flops 3764977664 | bytes 20447232 | tf_op jit(solution)/shard_map/dot_general | solution.py:60
  97.2 0.7 all-gather.8.cloned.1.call-update
  97.9 3.0 slice.8
  100.9 3.0 copy.22
  103.9 1.1 broadcast_in_dim.3
  105.1 2.5 fusion.14
  107.6 30.8 %all_to_all.20 = bf16[16,1,32,1024]{3,2,1,0:T(8,128)(2,1)S(1)} all-to-all(bf16[16,1,32,1024]{3,2,1,0:T(8,128)(2,1)S(1)} %fusion.14), channel_id=1, replica_groups=mesh['dp'=16,'tensor'=8] {'dp'}, dimensions={0} | all-to-all | bytes 2097152 | tf_op jit(solution)/shard_map/all_to_all | solution.py:27
  138.4 5.1 %all-to-all-start = ((bf16[256,16,256]{0,2,1:T(8,128)(2,1)}), bf16[256,16,256]{0,2,1:T(8,128)(2,1)S(1)}, u32[]{:S(2)}, u32[]{:S(2)}) async-start(bf16[256,16,256]{0,2,1:T(8,128)(2,1)} %bitcast), calls=%async_computation | async-start | bytes 4194304 | tf_op jit(solution)/shard_map/all_to_all | solution.py:53
  143.7 0.7 broadcast_multiply_fusion
  144.4 44.8 %all-to-all-done = bf16[256,16,256]{0,2,1:T(8,128)(2,1)S(1)} async-done(((bf16[256,16,256]{0,2,1:T(8,128)(2,1)}), bf16[256,16,256]{0,2,1:T(8,128)(2,1)S(1)}, u32[]{:S(2)}, u32[]{:S(2)}) %all-to-all-start) | async-done | bytes 2097184 | tf_op jit(solution)/shard_map/all_to_all | solution.py:53
  189.2 1.3 copy-done.2
  190.5 2.9 copy.21
  193.4 17.9 %all-gather.6.cloned.1.call-done = bf16[4096,1792]{1,0:T(8,128)(2,1)} async-done(((bf16[256,1792]{1,0:T(8,128)(2,1)}), bf16[4096,1792]{1,0:T(8,128)(2,1)}) %all-gather.6.cloned.1.call-update) | async-done | bytes 14680080 | tf_op jit(solution)/shard_map/all_gather | solution.py:80
  211.3 8.3 %convolution_convert_fusion.1 = bf16[256,1792]{1,0:T(8,128)(2,1)} fusion(bf16[4096,256]{1,0:T(8,128)(2,1)S(1)} %bitcast.26, bf16[4096,1792]{1,0:T(8,128)(2,1)} %all-gather.6.cloned.1.call-done), kind=kOutput, calls=%fused_computation.8 | convolution fusion | flops 3758555136 | bytes 17694720 | tf_op jit(solution)/shard_map/dot_general | solution.py:32
  219.6 76.5 %all-gather.8.cloned.1.call-done = bf16[4096,1792]{1,0:T(8,128)(2,1)} async-done(((bf16[256,1792]{1,0:T(8,128)(2,1)}), bf16[4096,1792]{1,0:T(8,128)(2,1)}) %all-gather.8.cloned.1.call-update) | async-done | bytes 14680080 | tf_op jit(solution)/shard_map/all_gather | solution.py:81
  296.2 8.5 %convolution_convert_fusion = bf16[256,1792]{1,0:T(8,128)(2,1)} fusion(bf16[4096,256]{1,0:T(8,128)(2,1)S(1)} %bitcast.27, bf16[4096,1792]{1,0:T(8,128)(2,1)} %all-gather.8.cloned.1.call-done), kind=kOutput, calls=%fused_computation.7 | convolution fusion | flops 3758555136 | bytes 17694720 | tf_op jit(solution)/shard_map/dot_general | solution.py:32
  304.6 1.2 copy-done
  305.8 2.6 fusion.15
  308.4 1.7 copy-done.1
  310.2 2.6 fusion.18
  (13 shorter events, 0.4 us)
Async XLA Ops:
  7.2 78.2 %copy-start.4 = (bf16[256,1792]{1,0:T(8,128)(2,1)S(1)}, bf16[256,1792]{1,0:T(8,128)(2,1)}, u32[]{:S(2)}) copy-start(bf16[256,1792]{1,0:T(8,128)(2,1)} %param.7) | copy-start | bytes 2752516
  7.2 78.2 %copy-start.3 = (bf16[256,1792]{1,0:T(8,128)(2,1)S(1)}, bf16[256,1792]{1,0:T(8,128)(2,1)}, u32[]{:S(2)}) copy-start(bf16[256,1792]{1,0:T(8,128)(2,1)} %param.6) | copy-start | bytes 2752516
  7.2 78.2 %all-gather.4.cloned.1.call-start = ((), (), s32[]{:S(2)}) async-start(), calls=%async_computation.2 | async-start | bytes 4718592 | tf_op jit(solution)/shard_map/all_gather | solution.py:12
  10.4 200.9 %all-gather.6.cloned.1.call-start = ((), (), s32[]{:S(2)}) async-start(), calls=%async_computation.3 | async-start | bytes 15597568 | tf_op jit(solution)/shard_map/all_gather | solution.py:80
  97.1 199.0 %all-gather.8.cloned.1.call-start = ((), (), s32[]{:S(2)}) async-start(), calls=%async_computation.4 | async-start | bytes 15597568 | tf_op jit(solution)/shard_map/all_gather | solution.py:81
  138.4 50.8 %all-to-all-start = ((bf16[256,16,256]{0,2,1:T(8,128)(2,1)}), bf16[256,16,256]{0,2,1:T(8,128)(2,1)S(1)}, u32[]{:S(2)}, u32[]{:S(2)}) async-start(bf16[256,16,256]{0,2,1:T(8,128)(2,1)} %bitcast), calls=%async_computation | async-start | bytes 4194304 | tf_op jit(solution)/shard_map/all_to_all | solution.py:53
  189.2 1.3 copy-start.2
  296.1 9.7 %copy-start = (bf16[4096,1792]{1,0:T(8,128)(2,1)S(1)}, bf16[4096,1792]{1,0:T(8,128)(2,1)}, u32[]{:S(2)}) copy-start(bf16[4096,1792]{1,0:T(8,128)(2,1)} %all-gather.6.cloned.1.call-done) | copy-start | bytes 44040196
  296.2 14.0 %copy-start.1 = (bf16[4096,1792]{1,0:T(8,128)(2,1)S(1)}, bf16[4096,1792]{1,0:T(8,128)(2,1)}, u32[]{:S(2)}) copy-start(bf16[4096,1792]{1,0:T(8,128)(2,1)} %all-gather.8.cloned.1.call-done) | copy-start | bytes 44040196
Sparse Core Ops, SparseCore 0:
  10.9 74.4 all-gather.3
  97.2 114.0 all-gather.5
  213.6 82.5 all-gather.7
where the time goes:
time: 320 us; the launch traced here: 319 us
  waiting for transfers between devices  215 us (67%)
  matrix products  36.2 us (11%)
  blocking collectives  30.8 us (10%)
  local copies, waits for them, and re-layouts  16.6 us (5%)
  between operations  13.8 us (4%)
  starting transfers between devices  5.23 us (2%)
    all_gather x1, waiting for transfers between devices, on_device(): up_sums = accumulate_one(lax.all_gather(up_grad, 'dp', axis=0, tiled=True))  76.5 us
    all_gather x1, waiting for transfers between devices, sent_together(): whole, at, outs = (lax.all_gather(both, axis, axis=dim, tiled=True), 0, [])  75 us
    all_to_all x1, waiting for transfers between devices, on_device(): lax.all_to_all(split, 'dp', split_axis=1, concat_axis=0, tiled=True)  44.8 us
    all_to_all x1, blocking collectives, summed_on_arrival(): lax.all_to_all(tiles, axis, split_axis=0, concat_axis=0, tiled=True)  30.8 us
    dot_general x4, matrix products, inner(): lax.dot_general(left, right, (((0,), (0,)), ((), ())), preferred_element_...  22 us
    all_gather x1, waiting for transfers between devices, on_device(): lax.all_gather(gate_grad, 'dp', axis=0, tiled=True)  17.9 us
    dot_general x1, matrix products, on_device(): lax.dot_general(grad_full, down_weight, (((1,), (1,)), ((), ())), preferr...  11.7 us
    unnamed x12, local copies, waits for them, and re-layouts  6.54 us
  transfers between devices with their start and end apart: 4, of which 4 were waited for; matrix products, arithmetic and copies ran while one was open for 7% of the time, Pallas kernels for 0%

commit v1 on v0

--- a/solution.py
+++ b/solution.py
@@ -5,6 +5,11 @@
 
 BLK = 1024
 HBLK = 896
+
+
+def gather_over(x, axis, dim):
+    sent = jnp.stack([x] * lax.axis_size(axis))
+    return jnp.concatenate(lax.all_to_all(sent, axis, 0, 0), axis=dim)
 
 
 def sent_together(arrays, axis, dim, along):
@@ -77,7 +82,7 @@
         factor = inner(own_cols, block_cols_h)
         return (wgrad, factor)
 
-    gate_sums = accumulate_one(lax.all_gather(gate_grad, "dp", axis=0, tiled=True))
+    gate_sums = accumulate_one(gather_over(gate_grad, "dp", 0))
     up_sums = accumulate_one(lax.all_gather(up_grad, "dp", axis=0, tiled=True))
     gate_wgrad = gate_sums[0].astype(jnp.bfloat16)
     up_wgrad = up_sums[0].astype(jnp.bfloat16)

time: 320 us -> 481 us (1.50)
  waiting for transfers between devices: 215 us -> 313 us
  blocking collectives: 30.8 us -> 83.9 us
  matrix products: 36.2 us -> 42.7 us
    all_to_all x1, waiting for transfers between devices: 44.8 us -> 238 us  [gather_over(): return jnp.concatenate(lax.all_to_all(sent, axis, 0, 0), axis=dim)]
    all_gather x1, waiting for transfers between devices: 76.5 us -> 0.01 us  [on_device(): up_sums = accumulate_one(lax.all_gather(up_grad, 'dp', axis=0, tiled=True))]
    all_to_all x0 -> x1, blocking collectives: none -> 53.1 us  [on_device(): lax.all_to_all(split, 'dp', split_axis=1, concat_axis=0, tiled=True)]
    all_gather x1 -> x0, waiting for transfers between devices: 17.9 us -> none  [on_device(): lax.all_gather(gate_grad, 'dp', axis=0, tiled=True)]
    another operation x0 -> x1, local copies, waits for them, and re-layouts: none -> 7.84 us  [gather_over(): sent = jnp.stack([x] * lax.axis_size(axis))]
    dot_general x4, matrix products: 22 us -> 29.5 us  [inner(): lax.dot_general(left, right, (((0,), (0,)), ((), ())), preferred_element_...]
  transfers between devices with their start and end apart: 4 -> 3, of which waited for: 4 -> 2; matrix products, arithmetic and copies ran while one was open for 7% -> 7% of each run, Pallas kernels for 0% -> 0%
where the time goes in v1:
time: 481 us; the launch traced here: 480 us
  waiting for transfers between devices  313 us (65%)
  blocking collectives  83.9 us (17%)
  matrix products  42.7 us (9%)
  local copies, waits for them, and re-layouts  19.9 us (4%)
  between operations  14.1 us (3%)
  starting transfers between devices  5.2 us (1%)
    all_to_all x1, waiting for transfers between devices, gather_over(): return jnp.concatenate(lax.all_to_all(sent, axis, 0, 0), axis=dim)  238 us
    all_gather x1, waiting for transfers between devices, sent_together(): whole, at, outs = (lax.all_gather(both, axis, axis=dim, tiled=True), 0, [])  75 us
    all_to_all x1, blocking collectives, on_device(): lax.all_to_all(split, 'dp', split_axis=1, concat_axis=0, tiled=True)  53.1 us
    all_to_all x1, blocking collectives, summed_on_arrival(): lax.all_to_all(tiles, axis, split_axis=0, concat_axis=0, tiled=True)  30.8 us
    dot_general x4, matrix products, inner(): lax.dot_general(left, right, (((0,), (0,)), ((), ())), preferred_element_...  29.5 us
    dot_general x1, matrix products, on_device(): lax.dot_general(grad_full, down_weight, (((1,), (1,)), ((), ())), preferr...  11.7 us
  transfers between devices with their start and end apart: 3, of which 2 were waited for; matrix products, arithmetic and copies ran while one was open for 7% of the time, Pallas kernels for 0%

profile of v1, /device:TPU:1, one launch (start us, length us, event | category | flops | bytes accessed | tf_op | source)
XLA Modules:
  0.0 480.1 jit_solution(3165291360729129092)
XLA Ops:
  7.2 0.0 all-gather.3.cloned.1.call-start
  7.2 1.2 copy.19
  8.4 1.1 copy.20
  9.5 0.8 pad_maximum_fusion
  10.4 0.0 all-gather.3.cloned.1.call-update
  10.4 0.0 all-gather.5.cloned.1.call-start
  10.4 75.0 %all-gather.3.cloned.1.call-done = bf16[512,4096]{0,1:T(8,128)(2,1)} async-done(((bf16[512,512]{0,1:T(8,128)(2,1)}), bf16[512,4096]{0,1:T(8,128)(2,1)}) %all-gather.3.cloned.1.call-update) | async-done | bytes 4194320 | tf_op jit(solution)/shard_map/all_gather | solution.py:17
  85.4 11.7 %fusion.13 = (bf16[256,1792]{1,0:T(8,128)(2,1)}, bf16[256,1792]{1,0:T(8,128)(2,1)}) fusion(bf16[256,1792]{1,0:T(8,128)(2,1)S(1)} %copy-done, bf16[256,1792]{1,0:T(8,128)(2,1)S(1)} %copy-done.1, bf16[1792,4096]{1,0:T(8,128)(2,1)} %param.9, bf16[512,4096]{0,1:T(8,128)(2,1)} %all-gather.3.cloned.1.call-done), kind=kOutput, calls=%fused_computation.19 | convolution fusion | flops 3764977664 | bytes 20447232 | tf_op jit(solution)/shard_map/dot_general | solution.py:65
  97.1 1.7 slice.8
  98.9 2.4 copy.22
  101.3 2.7 broadcast_in_dim.3
  104.0 1.5 fusion.14
  105.6 30.8 %all_to_all.25 = bf16[16,1,32,1024]{3,2,1,0:T(8,128)(2,1)S(1)} all-to-all(bf16[16,1,32,1024]{3,2,1,0:T(8,128)(2,1)S(1)} %fusion.14), channel_id=1, replica_groups=mesh['dp'=16,'tensor'=8] {'dp'}, dimensions={0} | all-to-all | bytes 2097152 | tf_op jit(solution)/shard_map/all_to_all | solution.py:32
  136.4 53.1 %all_to_all.26 = bf16[256,16,256]{0,2,1:T(8,128)(2,1)} all-to-all(bf16[256,16,256]{0,2,1:T(8,128)(2,1)S(1)} %bitcast.31), channel_id=1, replica_groups=mesh['dp'=16,'tensor'=8] {'dp'}, dimensions={1} | all-to-all | bytes 4194304 | tf_op jit(solution)/shard_map/all_to_all | solution.py:58
  189.5 7.8 %stack.2 = bf16[16,256,1792]{2,1,0:T(8,128)(2,1)} broadcast(bf16[256,1792]{1,0:T(8,128)(2,1)} %get-tuple-element.6), dimensions={1,2} | broadcast | bytes 15597568 | tf_op jit(solution)/shard_map/stack | solution.py:11
  197.3 5.1 %all-to-all-start.1 = ((bf16[16,256,1792]{2,1,0:T(8,128)(2,1)}), bf16[16,256,1792]{2,1,0:T(8,128)(2,1)}, u32[]{:S(2)}, u32[]{:S(2)}) async-start(bf16[16,256,1792]{2,1,0:T(8,128)(2,1)} %stack.2), calls=%async_computation.1 | async-start | bytes 29360128 | tf_op jit(solution)/shard_map/all_to_all | solution.py:12
  202.5 0.2 convert_reduce_fusion
  202.7 0.7 broadcast_multiply_fusion
  203.3 2.8 copy.21
  206.2 237.6 %all-to-all-done.1 = bf16[16,256,1792]{2,1,0:T(8,128)(2,1)} async-done(((bf16[16,256,1792]{2,1,0:T(8,128)(2,1)}), bf16[16,256,1792]{2,1,0:T(8,128)(2,1)}, u32[]{:S(2)}, u32[]{:S(2)}) %all-to-all-start.1) | async-done | bytes 14680096 | tf_op jit(solution)/shard_map/all_to_all | solution.py:12
  443.7 6.3 %fusion.15 = f32[1,112,896]{2,1,0:T(8,128)} fusion(bf16[4096,1792]{1,0:T(8,128)(2,1)} %bitcast.4, s32[]{:T(128)S(6)} %select_n.20, s32[]{:T(128)S(6)} %select_n.18), kind=kOutput, calls=%fused_computation.22 | convolution fusion | flops 822083584 | bytes 8790024 | tf_op jit(solution)/shard_map/dot_general | solution.py:37
  450.1 8.3 %convolution_convert_fusion.1 = bf16[256,1792]{1,0:T(8,128)(2,1)} fusion(bf16[4096,256]{1,0:T(8,128)(2,1)S(1)} %bitcast.27, bf16[4096,1792]{1,0:T(8,128)(2,1)} %bitcast.4), kind=kOutput, calls=%fused_computation.8 | convolution fusion | flops 3758555136 | bytes 17694720 | tf_op jit(solution)/shard_map/dot_general | solution.py:37
  458.4 6.5 %fusion.18 = f32[1,112,896]{2,1,0:T(8,128)} fusion(bf16[4096,1792]{1,0:T(8,128)(2,1)} %all-gather.5.cloned.1.call-done, s32[]{:T(128)S(6)} %select_n.20, s32[]{:T(128)S(6)} %select_n.18), kind=kOutput, calls=%fused_computation.23 | convolution fusion | flops 822083584 | bytes 8790024 | tf_op jit(solution)/shard_map/dot_general | solution.py:37
  464.9 8.3 %convolution_convert_fusion = bf16[256,1792]{1,0:T(8,128)(2,1)} fusion(bf16[4096,256]{1,0:T(8,128)(2,1)S(1)} %bitcast.28, bf16[4096,1792]{1,0:T(8,128)(2,1)} %all-gather.5.cloned.1.call-done), kind=kOutput, calls=%fused_computation.7 | convolution fusion | flops 3758555136 | bytes 17694720 | tf_op jit(solution)/shard_map/dot_general | solution.py:37
  (6 shorter events, 0.0 us)
Async XLA Ops:
  7.2 78.2 %copy-start.1 = (bf16[256,1792]{1,0:T(8,128)(2,1)S(1)}, bf16[256,1792]{1,0:T(8,128)(2,1)}, u32[]{:S(2)}) copy-start(bf16[256,1792]{1,0:T(8,128)(2,1)} %param.7) | copy-start | bytes 2752516
  7.2 78.2 %copy-start = (bf16[256,1792]{1,0:T(8,128)(2,1)S(1)}, bf16[256,1792]{1,0:T(8,128)(2,1)}, u32[]{:S(2)}) copy-start(bf16[256,1792]{1,0:T(8,128)(2,1)} %param.6) | copy-start | bytes 2752516
  7.2 78.2 %all-gather.3.cloned.1.call-start = ((), (), s32[]{:S(2)}) async-start(), calls=%async_computation.3 | async-start | bytes 4718592 | tf_op jit(solution)/shard_map/all_gather | solution.py:17
  10.4 448.0 %all-gather.5.cloned.1.call-start = ((), (), s32[]{:S(2)}) async-start(), calls=%async_computation.4 | async-start | bytes 15597568 | tf_op jit(solution)/shard_map/all_gather | solution.py:86
  197.3 246.4 %all-to-all-start.1 = ((bf16[16,256,1792]{2,1,0:T(8,128)(2,1)}), bf16[16,256,1792]{2,1,0:T(8,128)(2,1)}, u32[]{:S(2)}, u32[]{:S(2)}) async-start(bf16[16,256,1792]{2,1,0:T(8,128)(2,1)} %stack.2), calls=%async_computation.1 | async-start | bytes 29360128 | tf_op jit(solution)/shard_map/all_to_all | solution.py:12
Sparse Core Ops, SparseCore 0:
  10.9 74.4 all-gather.2
  97.2 117.9 all-gather.4
